TPU v7x, 256 devices: a whole 4x4x8 slice. The times are simulated.
256 devices in a mesh: sec: 4 (over y_lo, core), seq: 64 (over y_hi, z, x).
Axes of the slice: x: 4, y: 4 (y_hi: 2, y_lo: 2; y = y_hi * 2 + y_lo), z: 8, core: 2. Of those that a mesh axis runs over, the one named last changes fastest.
Arguments:
- embedded: bfloat16 [4, 8192, 2304], P('sec', 'seq'), may hold values from -6 to 6
- recent: bfloat16 [4, 3, 8192, 2304], P('sec', None, 'seq'), may hold values from -6 to 6
- query_depth: float32 [4, 2304], P('sec'), may hold values from -6 to 6
- depth_temp: float32 [4], P('sec'), may hold values from 24 to 80
- w_latent: bfloat16 [4, 2304, 512], P('sec'), may hold values from -0.125 to 0.125
- w_query: bfloat16 [4, 2304, 2048], P('sec', None, 'seq'), may hold values from -0.125 to 0.125
- w_uk: bfloat16 [4, 16, 128, 512], P('sec'), may hold values from -0.5 to 0.5
- attn_temp: float32 [4, 16], P('sec'), may hold values from 16 to 64
- w_uv: bfloat16 [4, 16, 512, 128], P('sec'), may hold values from -1 to 1
- w_out: bfloat16 [4, 2048, 2304], P('sec', 'seq'), may hold values from -0.25 to 0.25
- block_offsets: int32 [64], replicated, may hold values from 0 to 63, as said below
Outputs:
- block_out: bfloat16 [4, 8192, 2304], P('sec', 'seq')
Inputs may be any that keep to these rules, and one draw needn't show every extreme that they name: `block_offsets`: entries g * 64 to g * 64 + 63 hold every number of 0 to 63 once, for each sequence g.
All inputs are finite; a program needn't handle non-finite values.
Results may differ from a plain program's by a relative error of at most 0.012.
Values may be sent and summed in bfloat16 or wider, within the bound.
A program may use at most 128 MiB of HBM per device.

v0:
```python
import functools

import jax
import jax.numpy as jnp
from jax import lax
from jax.experimental import pallas as pl
from jax.experimental.pallas import tpu as pltpu
from jax.sharding import PartitionSpec as P

MESH = pl.DeviceIdType.MESH
EPS = 1e-06
NY, NZ, NX = 2, 8, 4
GROUP = NY * NZ


def place():
    sec = lax.axis_index("sec")
    seq = lax.axis_index("seq")
    return sec, seq // (NZ * NX), (seq // NX) % NZ, seq % NX


def seq_of(y, z, x):
    return (y * NZ + z) * NX + x


class Net:
    def __init__(self, ssem, rsem):
        self.ssem, self.rsem, self.count, self.sent = ssem, rsem, 0, []

    def number(self):
        self.count += 1
        return self.count - 1

    def copy(self, n, src, dst, dev):
        return pltpu.make_async_remote_copy(
            src_ref=src,
            dst_ref=dst,
            send_sem=self.ssem.at[n],
            recv_sem=self.rsem.at[n],
            device_id=dev,
            device_id_type=MESH,
        )

    def send(self, n, src, dst, dev):
        c = self.copy(n, src, dst, dev)
        c.start()
        self.sent.append(c)

    def got(self, n, dst, dev):
        self.copy(n, dst, dst, dev).wait_recv()

    def drain(self):
        for c in self.sent:
            c.wait_send()


def meet(devs):
    barrier = pltpu.get_barrier_semaphore()
    for d in devs:
        pl.semaphore_signal(barrier, inc=1, device_id=d, device_id_type=MESH)
    pl.semaphore_wait(barrier, len(devs))


def peers():
    sec, y, z, x = place()
    return dict(
        right=(sec, seq_of(y, z, (x + 1) % NX)),
        left=(sec, seq_of(y, z, (x + 3) % NX)),
        over=(sec, seq_of(y, z, (x + 2) % NX)),
        up=(sec, seq_of(y, (z + 1) % NZ, x)),
        down=(sec, seq_of(y, (z + 7) % NZ, x)),
        far=(sec, seq_of(1 - y, z, x)),
    )


def first_kernel(recent, wq, wo, relayed, wq_all, wo_all, ssem, rsem):
    sec, y, z, x = place()
    seq = seq_of(y, z, x)
    n_sec = lax.axis_size("sec")
    at = peers()
    group, rank = seq // GROUP, seq % GROUP
    owner = rank * NX + group
    source = x * GROUP + seq // NX
    mine = seq // NX
    barrier = pltpu.get_barrier_semaphore()
    for name in ("up", "down", "far"):
        pl.semaphore_signal(barrier, inc=1, device_id=at[name], device_id_type=MESH)
    for a in range(1, n_sec):
        pl.semaphore_signal(
            barrier, inc=1, device_id=(lax.rem(sec + a, n_sec), seq), device_id_type=MESH
        )
    away = owner != seq

    @pl.when(away)
    def _():
        pl.semaphore_signal(barrier, inc=1, device_id=(sec, source), device_id_type=MESH)

    pl.semaphore_wait(barrier, 3 + n_sec - 1 + away.astype(jnp.int32))

    net = Net(ssem, rsem)
    shifts = []
    for a in range(1, n_sec):
        n = net.number()
        ok = sec + a < n_sec
        c = net.copy(
            n, recent.at[a - 1], relayed.at[a - 1], (lax.rem(sec + a, n_sec), seq)
        )
        pl.when(ok)(c.start)
        shifts.append((a, ok, c, n))
    arrays = ((wq, wq_all, 0), (wo, wo_all, y * NZ))
    moves = []
    for i, (src, out, base) in enumerate(arrays):
        n = net.number()
        there = rank if i == 0 else lax.rem(rank, NZ)
        c = net.copy(n, src, out.at[there], (sec, owner))
        own = pltpu.make_async_copy(src, out.at[mine - base], ssem.at[n])
        pl.when(away)(c.start)
        pl.when(jnp.logical_not(away))(own.start)
        moves.append((out, n, c, own, base))
    right_n = {}
    left_n = {}
    far_n = {}
    for i, (out, n, c, own, base) in enumerate(moves):
        spot = out.at[mine - base]

        @pl.when(away)
        def _():
            net.copy(n, spot, spot, (sec, source)).wait_recv()

        pl.when(jnp.logical_not(away))(own.wait)
        if i == 0:
            far_n[i] = net.number()
            net.send(far_n[i], spot, spot, at["far"])
        right_n[i, 0, 1] = net.number()
        net.send(right_n[i, 0, 1], spot, spot, at["up"])
        left_n[i, 0, 1] = net.number()
        net.send(left_n[i, 0, 1], spot, spot, at["down"])
    for i, (out, n, c, own, base) in enumerate(moves[:1]):
        spot = out.at[(1 - y) * NZ + z]
        net.got(far_n[i], spot, at["far"])
        right_n[i, 1, 1] = net.number()
        net.send(right_n[i, 1, 1], spot, spot, at["up"])
        left_n[i, 1, 1] = net.number()
        net.send(left_n[i, 1, 1], spot, spot, at["down"])
    for k in range(1, 5):
        for i, (out, n, c, own, base) in enumerate(moves):
            for d in range(2):
                yy = y if d == 0 else 1 - y
                if (i, d, k) in right_n:
                    spot = out.at[yy * NZ - base + lax.rem(z + NZ - k, NZ)]
                    net.got(right_n[i, d, k], spot, at["down"])
                    if k < (4 if d == 0 else 3):
                        right_n[i, d, k + 1] = net.number()
                        net.send(right_n[i, d, k + 1], spot, spot, at["up"])
                if (i, d, k) in left_n:
                    spot = out.at[yy * NZ - base + lax.rem(z + k, NZ)]
                    net.got(left_n[i, d, k], spot, at["up"])
                    if k < (3 if d == 0 else 4):
                        left_n[i, d, k + 1] = net.number()
                        net.send(left_n[i, d, k + 1], spot, spot, at["down"])
    for a, ok, c, n in shifts:
        pl.when(ok)(c.wait_send)
        back = net.copy(
            n,
            relayed.at[a - 1],
            relayed.at[a - 1],
            (lax.rem(sec + n_sec - a, n_sec), seq),
        )
        pl.when(sec >= a)(back.wait_recv)
    for out, n, c, own, base in moves:
        pl.when(away)(c.wait_send)
    net.drain()


N_FIRST = 3 + 2 + 1 + 14 + 7


def first(recent, wq, wo):
    any_ = pl.BlockSpec(memory_space=pl.ANY)
    return pl.pallas_call(
        first_kernel,
        out_shape=(
            jax.ShapeDtypeStruct(recent.shape, recent.dtype),
            jax.ShapeDtypeStruct((GROUP,) + wq.shape, wq.dtype),
            jax.ShapeDtypeStruct((NZ,) + wo.shape, wo.dtype),
        ),
        in_specs=[any_] * 3,
        out_specs=(any_,) * 3,
        scratch_shapes=[
            pltpu.SemaphoreType.DMA((N_FIRST,)),
            pltpu.SemaphoreType.DMA((N_FIRST,)),
        ],
        compiler_params=pltpu.CompilerParams(collective_id=0, has_side_effects=True),
        name="shift_and_weights",
    )(recent, wq, wo)


def main_kernel(
    bo, temps, keys, mixed, wq, uk, uv, wo_half, out,
    mixed_v, wq_v, uk_v, kv, uv_v, wo_v, scaled, acc, den, ho, po, passing, landed,
    ssem, rsem, lsem,
):
    sec, y, z, x = place()
    at = peers()
    rows, lat = keys.shape
    heads, hdim, _ = uk.shape
    width = mixed.shape[1]
    group_rows = heads * rows
    half = rows // 2
    lo, hi = pl.ds(0, half), pl.ds(half, half)
    f32, bf = jnp.float32, jnp.bfloat16

    def slot(yy, zz, xx):
        return (yy * NZ + zz) * NX + xx

    def xs(i):
        return lax.rem(x + i, NX)

    me = slot(y, z, x)
    wo_mine = pl.ds(y * NZ, NZ)
    loads = [
        pltpu.make_async_copy(a, b, lsem.at[i])
        for i, (a, b) in enumerate(
            (
                (wq, wq_v),
                (uk, uk_v),
                (keys, kv.at[me]),
                (uv, uv_v),
                (wo_half, wo_v.at[wo_mine]),
            )
        )
    ]
    for c in loads[:3]:
        c.start()
    meet([at[n] for n in ("right", "left", "over", "up", "down", "far")])
    net = Net(ssem, rsem)
    up_n, down_n, bx, bxx, ax, mx = {}, {}, {}, {}, {}, {}

    def onward(kind, c, k, src, spot, ways=3):
        last_up = 4 if c % 2 == 0 else 3
        last_down = 7 - last_up
        if ways & 1 and k <= last_up:
            up_n[kind, c, k] = net.number()
            net.send(up_n[kind, c, k], src, spot, at["up"])
        if ways & 2 and k <= last_down:
            down_n[kind, c, k] = net.number()
            net.send(down_n[kind, c, k], src, spot, at["down"])

    def side(c, k, src, spot):
        for name in ("right", "left"):
            bx[c, k, name] = net.number()
            net.send(bx[c, k, name], src, spot, at[name])

    def relay(c, yy, zz, k):
        r = kv.at[slot(yy, zz, xs(3)), hi]
        l = kv.at[slot(yy, zz, xs(1)), hi]
        net.got(bx[c, k, "right"], r, at["left"])
        net.got(bx[c, k, "left"], l, at["right"])
        bxx[c, k] = net.number()
        if (c + k) % 2 == 0:
            net.send(bxx[c, k], r, r, at["right"])
        else:
            net.send(bxx[c, k], l, l, at["left"])

    def ended(c, yy, zz, k):
        spot = kv.at[slot(yy, zz, xs(2)), hi]
        net.got(bxx[c, k], spot, at["left"] if (c + k) % 2 == 0 else at["right"])

    def tile_of(c, tag):
        yy = y if c == 0 else 1 - y
        return c, yy, lax.rem(z + NZ - tag, NZ), tag

    a_x = {0: x, 1: xs(3), 2: xs(1), 3: xs(2)}

    def piece(k, c, way):
        table, back = (up_n, "down") if way == 1 else (down_n, "up")
        tag = k if way == 1 else -k
        _, yy, zz, _ = tile_of(c, tag)
        if ("b", c, k) in table:
            spot = kv.at[slot(yy, zz, x), hi]
            net.got(table["b", c, k], spot, at[back])
            onward("b", c, k + 1, spot, spot, way)
            side(c, tag, spot, spot)
        for i in range(NX):
            n = ("a", c * NX + i, k)
            if n in table:
                spot = kv.at[slot(yy, zz, a_x[i]), lo]
                net.got(table[n], spot, at[back])
                onward("a", c * NX + i, k + 1, spot, spot, way)
        if k > 1:
            relay(*tile_of(c, (k - 1) * (1 if way == 1 else -1)))
        elif way == 1:
            relay(*tile_of(c, 0))

    for name in ("right", "left", "over"):
        ax[name] = net.number()
        net.send(ax[name], keys.at[lo], kv.at[me, lo], at[name])
    b_far = net.number()
    net.send(b_far, keys.at[hi], kv.at[me, hi], at["far"])
    a_far = [net.number() for _ in range(NX)]
    net.send(a_far[0], keys.at[lo], kv.at[me, lo], at["far"])
    onward("b", 0, 1, keys.at[hi], kv.at[me, hi])
    onward("a", 0, 1, keys.at[lo], kv.at[me, lo])
    for name in ("right", "left"):
        for h, part in ((0, lo), (1, hi)):
            if name == "left":
                h, part = 1 - h, (hi, lo)[h]
            mx[name, h] = net.number()
            net.send(mx[name, h], mixed.at[part], mixed_v.at[x, part], at[name])
    side(0, 0, keys.at[hi], kv.at[me, hi])
    for i, (name, back) in enumerate(
        (("right", "left"), ("left", "right"), ("over", "over")), start=1
    ):
        spot = kv.at[slot(y, z, a_x[i]), lo]
        net.got(ax[name], spot, at[back])
        net.send(a_far[i], spot, spot, at["far"])
        onward("a", i, 1, spot, spot)
    spot = kv.at[slot(1 - y, z, x), hi]
    net.got(b_far, spot, at["far"])
    onward("b", 1, 1, spot, spot)
    side(1, 0, spot, spot)
    for i in range(NX):
        spot = kv.at[slot(1 - y, z, a_x[i]), lo]
        net.got(a_far[i], spot, at["far"])
        onward("a", NX + i, 1, spot, spot)
    wo_far = net.number()
    net.send(wo_far, wo_half, wo_v.at[wo_mine], at["far"])
    for c in loads[3:]:
        c.start()

    for c in loads[:3]:
        c.wait()
    acc[...] = jnp.zeros_like(acc)
    den[...] = jnp.zeros_like(den)
    weights = wq_v[...].reshape(heads * hdim, width)

    def ask(b, source):
        q = lax.dot_general(
            source, weights, (((1,), (1,)), ((), ())), preferred_element_type=f32
        ).astype(bf)
        for h in range(heads):
            a = jnp.dot(q[:, h * hdim:(h + 1) * hdim], uk_v[h], preferred_element_type=f32)
            r = lax.rsqrt(jnp.mean(a * a, axis=-1, keepdims=True) + EPS)
            scaled[b, pl.ds(h * rows, rows), :] = (a * r * temps[h] / lat).astype(bf)

    gap = lax.broadcasted_iota(jnp.int32, (rows, rows), 1) - lax.broadcasted_iota(
        jnp.int32, (rows, rows), 0
    )

    def task(b, yy, zz):
        base = slot(yy, zz, 0)
        k = kv[pl.ds(base, NX)].reshape(NX * rows, lat)
        here = bo[slot(y, z, b)]
        limit = [(here - bo[base + j]) * rows for j in range(NX)]
        seen = [gap <= limit[j] for j in range(NX)]
        n_h = 2
        for h0 in range(0, heads, n_h):
            part = pl.ds(h0 * rows, n_h * rows)
            s = lax.dot_general(
                scaled[b, part, :], k, (((1,), (1,)), ((), ())), preferred_element_type=f32
            )
            p = jnp.exp(s)
            p = jnp.concatenate(
                [
                    jnp.concatenate(
                        [
                            jnp.where(
                                seen[j],
                                p[h * rows:(h + 1) * rows, j * rows:(j + 1) * rows],
                                0.0,
                            )
                            for j in range(NX)
                        ],
                        axis=1,
                    )
                    for h in range(n_h)
                ],
                axis=0,
            )
            d = p[:, 0:rows]
            for j in range(1, NX):
                d = d + p[:, j * rows:(j + 1) * rows]
            den[b, part, :] += d
            acc[b, part, :] += jnp.dot(p.astype(bf), k, preferred_element_type=f32)

    def first_tiles(b):
        def one(i, _):
            task(b, y + i * (1 - 2 * y), z)
            return 0

        lax.fori_loop(0, 2, one, 0)

    ask(x, mixed[...])
    piece(1, 0, 1)
    piece(1, 0, 2)
    piece(1, 1, 1)
    piece(1, 1, 2)
    spot = mixed_v.at[xs(3), lo]
    net.got(mx["right", 0], spot, at["left"])
    m_up = net.number()
    net.send(m_up, spot, spot, at["right"])
    spot = mixed_v.at[xs(1), hi]
    net.got(mx["left", 1], spot, at["right"])
    m_down = net.number()
    net.send(m_down, spot, spot, at["left"])
    ended(*tile_of(0, 0))
    ended(*tile_of(1, 0))
    first_tiles(x)
    net.got(mx["right", 1], mixed_v.at[xs(3), hi], at["left"])
    net.got(mx["left", 0], mixed_v.at[xs(1), lo], at["right"])
    for i in (3, 1):
        ask(xs(i), mixed_v[xs(i)])
        first_tiles(xs(i))
        piece(2, 0, 1 if i == 3 else 2)
    net.got(m_up, mixed_v.at[xs(2), lo], at["left"])
    net.got(m_down, mixed_v.at[xs(2), hi], at["right"])
    ask(xs(2), mixed_v[xs(2)])
    first_tiles(xs(2))

    turns = [(c, w) for c in range(2) for w in (1, 2)]
    plan = [(2, 1, 1), (2, 1, 2)]
    plan += [(3, c, w) for c, w in turns]
    plan += [(4, 0, 1), (4, 0, 2), (4, 1, 1), (4, 1, 2)]
    plan_at = 0
    for k in (1, 2):
        for j, (c, w) in enumerate(turns):
            take = 2 if k == 1 and j == 0 else 1
            for _ in range(take):
                if plan_at < len(plan):
                    piece(*plan[plan_at])
                    plan_at += 1
            tag = k if w == 1 else -k
            ended(*tile_of(c, tag))
            _, yy, zz, _ = tile_of(c, tag)

            def one(b, _, yy=yy, zz=zz):
                task(b, yy, zz)
                return 0

            lax.fori_loop(0, NX, one, 0)
    while plan_at < len(plan):
        piece(*plan[plan_at])
        plan_at += 1
    last = [(0, 4), (1, -4)]
    for c, tag in last:
        relay(*tile_of(c, tag))
    for c, w in turns:
        ended(*tile_of(c, 3 if w == 1 else -3))
    for c, tag in last:
        ended(*tile_of(c, tag))

    def last_tiles(b):
        def one(i, _):
            task(b, y + (i % 2) * (1 - 2 * y), lax.rem(z + 3 + i // 2, NZ))
            return 0

        lax.fori_loop(0, 6, one, 0)
        for h in range(heads):
            part = pl.ds(h * rows, rows)
            d = jnp.sum(den[b, part, :], axis=-1, keepdims=True)
            ctx = (acc[b, part, :] / d).astype(bf)
            ho[:, h * hdim:(h + 1) * hdim] = jnp.dot(
                ctx, uv_v[h], preferred_element_type=f32
            ).astype(bf)

    def project():
        return jnp.dot(
            ho[...], wo_v[...].reshape(heads * hdim, width), preferred_element_type=f32
        )

    loads[3].wait()
    last_tiles(xs(2))
    loads[4].wait()
    net.got(wo_far, wo_v.at[pl.ds((1 - y) * NZ, NZ)], at["far"])
    po[0] = project().astype(bf)
    out_n = [net.number() for _ in range(4)]
    net.send(out_n[0], po.at[0, lo], passing.at[0], at["right"])
    net.send(out_n[1], po.at[0, hi], passing.at[1], at["left"])
    last_tiles(xs(1))
    net.got(out_n[0], passing.at[0], at["left"])
    res = project()
    po[1, lo] = (res[:half] + passing[0].astype(f32)).astype(bf)
    po[1, hi] = res[half:].astype(bf)
    net.send(out_n[2], po.at[1], landed.at[0], at["right"])
    last_tiles(xs(3))
    net.got(out_n[1], passing.at[1], at["right"])
    res = project()
    po[2, lo] = res[:half].astype(bf)
    po[2, hi] = (res[half:] + passing[1].astype(f32)).astype(bf)
    net.send(out_n[3], po.at[2], landed.at[1], at["left"])
    last_tiles(x)
    res = project()
    net.got(out_n[2], landed.at[0], at["left"])
    net.got(out_n[3], landed.at[1], at["right"])
    out[...] = (res + landed[0].astype(f32) + landed[1].astype(f32)).astype(out.dtype)
    net.drain()
    assert net.count == N_MAIN, net.count


N_MAIN = 3 + 4 + 56 + 1 + 14 + 48 + 6 + 1 + 4


def main(bo, temps, keys, mixed, wq, uk, uv, wo_half):
    rows, width = mixed.shape
    heads, hdim, lat = uk.shape
    any_ = pl.BlockSpec(memory_space=pl.ANY)
    smem = pl.BlockSpec(memory_space=pltpu.SMEM)
    vmem = pl.BlockSpec(memory_space=pltpu.VMEM)
    bf, f32 = jnp.bfloat16, jnp.float32
    n_dev = bo.shape[0]
    return pl.pallas_call(
        main_kernel,
        out_shape=jax.ShapeDtypeStruct((rows, width), bf),
        in_specs=[smem, smem, vmem, vmem, any_, any_, any_, any_],
        out_specs=vmem,
        scratch_shapes=[
            pltpu.VMEM((NX, rows, width), bf),
            pltpu.VMEM(wq.shape, bf),
            pltpu.VMEM(uk.shape, bf),
            pltpu.VMEM((n_dev, rows, lat), bf),
            pltpu.VMEM(uv.shape, bf),
            pltpu.VMEM((GROUP,) + wo_half.shape[1:], bf),
            pltpu.VMEM((NX, heads * rows, lat), bf),
            pltpu.VMEM((NX, heads * rows, lat), f32),
            pltpu.VMEM((NX, heads * rows, rows), f32),
            pltpu.VMEM((rows, heads * hdim), bf),
            pltpu.VMEM((3, rows, width), bf),
            pltpu.VMEM((2, rows // 2, width), bf),
            pltpu.VMEM((2, rows, width), bf),
            pltpu.SemaphoreType.DMA((N_MAIN,)),
            pltpu.SemaphoreType.DMA((N_MAIN,)),
            pltpu.SemaphoreType.DMA((5,)),
        ],
        compiler_params=pltpu.CompilerParams(
            collective_id=1, has_side_effects=True, vmem_limit_bytes=60 << 20
        ),
        name="attend_and_sum",
    )(bo, temps, keys, mixed, wq, uk, uv, wo_half)


def mix(embedded, relayed, sec, probe, temp):
    n = relayed.shape[0]
    ok = jnp.concatenate(
        [jnp.ones((1,), jnp.bool_), sec >= jnp.arange(1, n + 1, dtype=jnp.int32)]
    )
    stack = jnp.concatenate([embedded[None], relayed], axis=0)
    values = jnp.where(ok[:, None, None], stack, jnp.zeros_like(stack)).astype(jnp.float32)
    scale = lax.rsqrt(jnp.mean(probe * probe) + EPS) / probe.shape[0]
    norm = lax.rsqrt(jnp.mean(values * values, axis=-1) + EPS)
    logits = temp * scale * jnp.sum(values * probe, axis=-1) * norm
    weights = jnp.where(ok[:, None], jnp.exp(logits), 0.0)
    total = jnp.sum(weights, axis=0)
    return (jnp.sum(weights[..., None] * values, axis=0) / total[:, None]).astype(
        jnp.bfloat16
    )


def shards(
    embedded, recent, query_depth, depth_temp, w_latent, w_query, w_uk, attn_temp, w_uv,
    w_out, block_offsets,
):
    sec, y, z, x = place()
    relayed, wq_all, wo_half = first(recent[0], jnp.swapaxes(w_query[0], 0, 1), w_out[0])
    mixed = mix(embedded[0], relayed, sec, query_depth[0], depth_temp[0])
    latent = jnp.dot(mixed, w_latent[0], preferred_element_type=jnp.float32)
    keys = (
        latent * lax.rsqrt(jnp.mean(latent * latent, axis=-1, keepdims=True) + EPS)
    ).astype(jnp.bfloat16)
    heads = w_uk.shape[1] // NX
    pick = functools.partial(lax.dynamic_slice_in_dim, start_index=x * heads, slice_size=heads)
    return main(
        block_offsets, pick(attn_temp[0]), keys, mixed, wq_all, pick(w_uk[0]),
        pick(w_uv[0]), wo_half,
    )[None]


def solution(mesh):
    in_specs = (
        P("sec", "seq", None),
        P("sec", None, "seq", None),
        P("sec", None),
        P("sec"),
        P("sec", None, None),
        P("sec", None, "seq"),
        P("sec", None, None, None),
        P("sec", None),
        P("sec", None, None, None),
        P("sec", "seq", None),
        P(),
    )
    return jax.shard_map(
        shards, mesh=mesh, in_specs=in_specs, out_specs=P("sec", "seq", None), check_vma=False
    )
```

profile of v0, /device:TPU:16, one launch (start us, length us, event | category | flops | bytes accessed | tf_op | source)
XLA Modules:
  0.0 207.1 jit_solution(3471929797773410543)
XLA Ops:
  0.0 0.0 copy-start
  0.0 0.0 copy-start.2
  0.0 76.3 %shift_and_weights.1 = (bf16[3,128,2304]{2,1,0:T(8,128)(2,1)}, bf16[16,32,2304]{2,1,0:T(8,128)(2,1)}, bf16[8,32,2304]{2,1,0:T(8,128)(2,1)}) custom-call(bf16[3,128,2304]{2,1,0:T(8,128)(2,1)} %bitcast.21, bf16[32,2304]{1,0:T(8,128)(2,1)} %bitcast.22, bf16[32,2304]{1,0:T(8,128)(2,1)} %bitcast.23), custom_call_target="tpu_custom_call" | custom-call | tf_op jit(solution)/shard_map/shift_and_weights/pallas_call | solution.py:180
  76.4 0.1 pad_add_fusion
  76.4 0.7 reduce
  77.2 0.0 copy-done.2
  77.2 3.9 %fusion = (f32[4,128]{1,0:T(4,128)S(1)}, f32[4,128]{1,0:T(4,128)S(1)}, bf16[4,128,2304]{2,1,0:T(8,128)(2,1)}) fusion(f32[2304]{0:T(1024)S(1)} %reduce, bf16[3,128,2304]{2,1,0:T(8,128)(2,1)} %get-tuple-element.8, bf16[1,128,2304]{2,1,0:T(8,128)(2,1)S(1)} %copy-done.2, pred[4]{0:T(512)(128)(4,1)S(1)} %pad_add_fusion), kind=kLoop, calls=%fused_computation.3 | loop fusion | flops 8256512 | bytes 4731908 | tf_op jit(solution)/shard_map/reduce_sum | solution.py:550
  81.1 0.6 multiply_reduce_fusion.1
  83.1 0.1 fusion.6
  83.2 2.3 %fusion.2 = f32[128,2304]{1,0:T(8,128)S(1)} fusion(bf16[4,128,2304]{2,1,0:T(8,128)(2,1)} %get-tuple-element.15, f32[4,128]{1,0:T(4,128)S(1)} %get-tuple-element.14), kind=kLoop, calls=%fused_computation.5 | loop fusion | flops 3244032 | bytes 3540992 | tf_op jit(solution)/shard_map/reduce_sum | solution.py:553
  85.5 0.1 divide_convert_fusion.mixed
  85.6 0.0 copy-done
  85.6 0.0 copy-start.1
  85.7 0.0 copy-start.3
  85.7 0.6 multiply_reduce_fusion
  86.2 0.8 multiply_convert_fusion.keys
  87.0 1.9 dynamic-slice_bitcast_fusion.uv
  88.9 1.9 dynamic-slice_bitcast_fusion.1.uk
  90.7 0.0 copy-done.1
  90.7 0.0 copy-done.3
  90.7 0.6 fusion.5.temps
  91.4 113.8 %attend_and_sum.1 = bf16[128,2304]{1,0:T(8,128)(2,1)} custom-call(s32[64]{0:T(128)} %bo.1, f32[4]{0:T(128)} %fusion.5.temps, bf16[128,512]{1,0:T(8,128)(2,1)} %multiply_convert_fusion.keys, bf16[128,2304]{1,0:T(8,128)(2,1)} %copy-done.1, bf16[16,32,2304]{2,1,0:T(8,128)(2,1)} %get-tuple-element.9.wq, bf16[4,128,512]{2,1,0:T(8,128)(2,1)} %dynamic-slice_bitcast_fusion.1.uk, ...), custom_call_target="tpu_custom_call" | custom-call | tf_op jit(solution)/shard_map/attend_and_sum/pallas_call | solution.py:511
  205.2 1.9 copy.14
  (2 shorter events, 0.0 us)
Async XLA Ops:
  0.0 85.6 %copy-start = (bf16[1,2304,512]{2,1,0:T(8,128)(2,1)S(1)}, bf16[1,2304,512]{2,1,0:T(8,128)(2,1)}, u32[]{:S(2)}) copy-start(bf16[1,2304,512]{2,1,0:T(8,128)(2,1)} %param.15) | copy-start | bytes 7077892
  0.0 77.2 %copy-start.2 = (bf16[1,128,2304]{2,1,0:T(8,128)(2,1)S(1)}, bf16[1,128,2304]{2,1,0:T(8,128)(2,1)}, u32[]{:S(2)}) copy-start(bf16[1,128,2304]{2,1,0:T(8,128)(2,1)} %param.11) | copy-start | bytes 1769476
  85.6 5.1 %copy-start.1 = (bf16[128,2304]{1,0:T(8,128)(2,1)}, bf16[128,2304]{1,0:T(8,128)(2,1)S(1)}, u32[]{:S(2)}) copy-start(bf16[128,2304]{1,0:T(8,128)(2,1)S(1)} %divide_convert_fusion.mixed) | copy-start | bytes 1769476
  85.7 5.1 %copy-start.3 = (f32[1,16]{1,0:T(1,128)S(1)}, f32[1,16]{1,0:T(1,128)}, u32[]{:S(2)}) copy-start(f32[1,16]{1,0:T(1,128)} %param.18) | copy-start | bytes 196
where the time goes:
time: 209 us; the launch traced here: 207 us
  Pallas kernels  190 us (91%)
  other arithmetic  8.66 us (4%)
  local copies, waits for them, and re-layouts  6.31 us (3%)
    pallas_call x1, Pallas kernels, main(): pl.pallas_call(main_kernel, out_shape=jax.ShapeDtypeStruct((rows, width),...  114 us
    pallas_call x1, Pallas kernels, first(): pl.pallas_call(first_kernel, out_shape=(jax.ShapeDtypeStruct(recent.shape...  76.3 us

commit v1 on v0

v1 whole, which is shorter than its diff:
```python
import functools

import jax
import jax.numpy as jnp
from jax import lax
from jax.experimental import pallas as pl
from jax.experimental.pallas import tpu as pltpu
from jax.sharding import PartitionSpec as P

MESH = pl.DeviceIdType.MESH
EPS = 1e-06
NY, NZ, NX = 2, 8, 4
GROUP = NY * NZ


def place():
    sec = lax.axis_index("sec")
    seq = lax.axis_index("seq")
    return sec, seq // (NZ * NX), (seq // NX) % NZ, seq % NX


def seq_of(y, z, x):
    return (y * NZ + z) * NX + x


class Net:
    def __init__(self, ssem, rsem):
        self.ssem, self.rsem, self.count, self.sent = ssem, rsem, 0, []

    def number(self):
        self.count += 1
        return self.count - 1

    def copy(self, n, src, dst, dev):
        return pltpu.make_async_remote_copy(
            src_ref=src,
            dst_ref=dst,
            send_sem=self.ssem.at[n],
            recv_sem=self.rsem.at[n],
            device_id=dev,
            device_id_type=MESH,
        )

    def send(self, n, src, dst, dev, like=None):
        self.copy(n, src, dst, dev).start()
        self.sent.append((n, src if like is None else like))

    def got(self, n, dst, dev):
        self.copy(n, dst, dst, dev).wait_recv()

    def drain(self, dev):
        for n, like in self.sent:
            self.copy(n, like, like, dev).wait_send()


def peers():
    sec, y, z, x = place()
    return dict(
        right=(sec, seq_of(y, z, (x + 1) % NX)),
        left=(sec, seq_of(y, z, (x + 3) % NX)),
        over=(sec, seq_of(y, z, (x + 2) % NX)),
        up=(sec, seq_of(y, (z + 1) % NZ, x)),
        down=(sec, seq_of(y, (z + 7) % NZ, x)),
        far=(sec, seq_of(1 - y, z, x)),
    )


def tick_kernel(
    bo, temps, depth_temp, embedded, probe, wq, wo, recent, w_latent, w_uk, w_uv, out,
    relayed, blend, weight, lat_v, wq_v, wo_v, uk_v, uv_v, mixed_v, kv,
    scaled, acc, den, ho, po, passing, landed, ssem, rsem, lsem,
):
    sec, y, z, x = place()
    seq = slot_me = seq_of(y, z, x)
    n_sec = lax.axis_size("sec")
    at = peers()
    rows, width = embedded.shape
    _, hdim, lat = w_uk.shape
    heads = w_uk.shape[0] // NX
    half = rows // 2
    lo, hi = pl.ds(0, half), pl.ds(half, half)
    f32, bf = jnp.float32, jnp.bfloat16

    def slot(yy, zz, xx):
        return (yy * NZ + zz) * NX + xx

    def xs(i):
        return lax.rem(x + i, NX)

    mine_heads = pl.ds(x * heads, heads)
    loads = [
        pltpu.make_async_copy(a, b, lsem.at[i])
        for i, (a, b) in enumerate(
            ((w_latent, lat_v), (w_uk.at[mine_heads], uk_v), (w_uv.at[mine_heads], uv_v))
        )
    ]
    for c in loads:
        c.start()

    group, rank = seq // GROUP, seq % GROUP
    owner = rank * NX + group
    source = x * GROUP + seq // NX
    mine = seq // NX
    away = owner != seq
    barrier = pltpu.get_barrier_semaphore()
    names = ("right", "left", "over", "up", "down", "far")
    for name in names:
        pl.semaphore_signal(barrier, inc=1, device_id=at[name], device_id_type=MESH)
    for a in range(1, n_sec):
        pl.semaphore_signal(
            barrier, inc=1, device_id=(lax.rem(sec + a, n_sec), seq), device_id_type=MESH
        )

    @pl.when(away)
    def _():
        pl.semaphore_signal(barrier, inc=1, device_id=(sec, source), device_id_type=MESH)

    pl.semaphore_wait(barrier, len(names) + n_sec - 1 + away.astype(jnp.int32))

    net = Net(ssem, rsem)

    moves = []
    for i, (src, dst, base, there) in enumerate(
        ((wq, wq_v, 0, rank), (wo, wo_v, 0, rank))
    ):
        n = net.number()
        c = net.copy(n, src, dst.at[there], (sec, owner))
        own = pltpu.make_async_copy(src, dst.at[mine], ssem.at[n])
        pl.when(away)(c.start)
        pl.when(jnp.logical_not(away))(own.start)
        moves.append((dst, n, c, own))
    shifts = []
    for a in range(1, n_sec):
        n = net.number()
        ok = sec + a < n_sec
        c = net.copy(
            n, recent.at[a - 1], relayed.at[a - 1], (lax.rem(sec + a, n_sec), seq)
        )
        pl.when(ok)(c.start)
        shifts.append((a, ok, c, n))
    ring_up, ring_down = {}, {}

    def ring(i, d, k, spot, ways=3):
        last_up = 4 if d == 0 else 3
        if ways & 1 and k <= last_up:
            ring_up[i, d, k] = net.number()
            net.send(ring_up[i, d, k], spot, spot, at["up"])
        if ways & 2 and k <= 7 - last_up:
            ring_down[i, d, k] = net.number()
            net.send(ring_down[i, d, k], spot, spot, at["down"])

    def ring_step(k):
        for i, (dst, n, c, own) in enumerate(moves):
            for d in range(2):
                yy = y if d == 0 else 1 - y
                if (i, d, k) in ring_up:
                    spot = dst.at[yy * NZ + lax.rem(z + NZ - k, NZ)]
                    net.got(ring_up[i, d, k], spot, at["down"])
                    ring(i, d, k + 1, spot, 1)
                if (i, d, k) in ring_down:
                    spot = dst.at[yy * NZ + lax.rem(z + k, NZ)]
                    net.got(ring_down[i, d, k], spot, at["up"])
                    ring(i, d, k + 1, spot, 2)

    q_far = net.number()
    for i, (dst, n, c, own) in enumerate(moves):
        spot = dst.at[mine]

        @pl.when(away)
        def _():
            net.copy(n, spot, spot, (sec, source)).wait_recv()

        pl.when(jnp.logical_not(away))(own.wait)
        if i == 0:
            net.send(q_far, spot, spot, at["far"])
        ring(i, 0, 1, spot)
    spot = wq_v.at[(1 - y) * NZ + z]
    net.got(q_far, spot, at["far"])
    ring(0, 1, 1, spot)
    ring_step(1)

    asked = probe[...]
    scale = (
        depth_temp[0] * lax.rsqrt(jnp.mean(asked * asked, axis=-1, keepdims=True) + EPS) / width
    )
    step_rows = 16

    def add_source(read, fresh):
        def some(i, _):
            part = pl.ds(pl.multiple_of(i * step_rows, step_rows), step_rows)
            v = read(part).astype(f32)
            norm = lax.rsqrt(jnp.mean(v * v, axis=-1, keepdims=True) + EPS)
            w = jnp.exp(scale * jnp.sum(v * asked, axis=-1, keepdims=True) * norm)
            if fresh:
                blend[part, :] = w * v
                weight[part, :] = jnp.broadcast_to(w, (step_rows, 128))
            else:
                blend[part, :] += w * v
                weight[part, :] += jnp.broadcast_to(w, (step_rows, 128))
            return 0

        lax.fori_loop(0, rows // step_rows, some, 0)

    add_source(lambda part: embedded[part, :], True)
    ring_step(2)
    for a, ok, c, n in shifts:

        @pl.when(sec >= a)
        def _():
            net.copy(
                n,
                relayed.at[a - 1],
                relayed.at[a - 1],
                (lax.rem(sec + n_sec - a, n_sec), seq),
            ).wait_recv()
            add_source(lambda part: relayed[a - 1, part, :], False)

    def finish(i, _):
        part = pl.ds(pl.multiple_of(i * step_rows, step_rows), step_rows)
        mixed_v[x, part, :] = (blend[part, :] / weight[part, 0:1]).astype(bf)
        return 0

    lax.fori_loop(0, rows // step_rows, finish, 0)
    loads[0].wait()
    latent = jnp.dot(mixed_v[x], lat_v[...], preferred_element_type=f32)
    kv[slot_me] = (
        latent * lax.rsqrt(jnp.mean(latent * latent, axis=-1, keepdims=True) + EPS)
    ).astype(bf)

    up_n, down_n, bx, bxx, ax, mx = {}, {}, {}, {}, {}, {}
    some_half = kv.at[0, lo]

    def onward(kind, c, k, spot, ways=3):
        last_up = 4 if c % 2 == 0 else 3
        if ways & 1 and k <= last_up:
            up_n[kind, c, k] = net.number()
            net.send(up_n[kind, c, k], spot, spot, at["up"], some_half)
        if ways & 2 and k <= 7 - last_up:
            down_n[kind, c, k] = net.number()
            net.send(down_n[kind, c, k], spot, spot, at["down"], some_half)

    def side(c, k, spot):
        for name in ("right", "left"):
            bx[c, k, name] = net.number()
            net.send(bx[c, k, name], spot, spot, at[name], some_half)

    def tile_of(c, tag):
        yy = y if c == 0 else 1 - y
        return c, yy, lax.rem(z + NZ - tag, NZ), tag

    def relay(c, tag):
        _, yy, zz, _ = tile_of(c, tag)
        r = kv.at[slot(yy, zz, xs(3)), hi]
        l = kv.at[slot(yy, zz, xs(1)), hi]
        net.got(bx[c, tag, "right"], r, at["left"])
        net.got(bx[c, tag, "left"], l, at["right"])
        bxx[c, tag] = net.number()
        if (c + tag) % 2 == 0:
            net.send(bxx[c, tag], r, r, at["right"], some_half)
        else:
            net.send(bxx[c, tag], l, l, at["left"], some_half)

    def ended(c, tag):
        _, yy, zz, _ = tile_of(c, tag)
        spot = kv.at[slot(yy, zz, xs(2)), hi]
        net.got(bxx[c, tag], spot, at["left"] if (c + tag) % 2 == 0 else at["right"])

    a_x = {0: x, 1: xs(3), 2: xs(1), 3: xs(2)}

    def piece(k, c, way):
        table, back = (up_n, "down") if way == 1 else (down_n, "up")
        tag = k if way == 1 else -k
        _, yy, zz, _ = tile_of(c, tag)
        if ("b", c, k) in table:
            spot = kv.at[slot(yy, zz, x), hi]
            net.got(table["b", c, k], spot, at[back])
            onward("b", c, k + 1, spot, way)
            side(c, tag, spot)
        for i in range(NX):
            n = ("a", c * NX + i, k)
            if n in table:
                spot = kv.at[slot(yy, zz, a_x[i]), lo]
                net.got(table[n], spot, at[back])
                onward("a", c * NX + i, k + 1, spot, way)

    ring_step(3)
    mine_lo, mine_hi = kv.at[slot_me, lo], kv.at[slot_me, hi]
    for name in ("right", "left", "over"):
        ax[name] = net.number()
        net.send(ax[name], mine_lo, mine_lo, at[name])
    b_far = net.number()
    net.send(b_far, mine_hi, mine_hi, at["far"])
    a_far = [net.number() for _ in range(NX)]
    net.send(a_far[0], mine_lo, mine_lo, at["far"])
    onward("b", 0, 1, mine_hi)
    onward("a", 0, 1, mine_lo)
    for name in ("right", "left"):
        for h in (0, 1) if name == "right" else (1, 0):
            mx[name, h] = net.number()
            spot = mixed_v.at[x, (lo, hi)[h]]
            net.send(mx[name, h], spot, spot, at[name])
    side(0, 0, mine_hi)
    for i, (name, back) in enumerate(
        (("right", "left"), ("left", "right"), ("over", "over")), start=1
    ):
        spot = kv.at[slot(y, z, a_x[i]), lo]
        net.got(ax[name], spot, at[back])
        net.send(a_far[i], spot, spot, at["far"])
        onward("a", i, 1, spot)
    spot = kv.at[slot(1 - y, z, x), hi]
    net.got(b_far, spot, at["far"])
    onward("b", 1, 1, spot)
    side(1, 0, spot)
    for i in range(NX):
        spot = kv.at[slot(1 - y, z, a_x[i]), lo]
        net.got(a_far[i], spot, at["far"])
        onward("a", NX + i, 1, spot)
    ring_step(4)
    wo_far = net.number()
    wo_mine, wo_other = pl.ds(y * NZ, NZ), pl.ds((1 - y) * NZ, NZ)
    net.send(wo_far, wo_v.at[wo_mine], wo_v.at[wo_mine], at["far"])

    loads[1].wait()
    acc[...] = jnp.zeros_like(acc)
    den[...] = jnp.zeros_like(den)

    def ask(b):
        q = lax.dot_general(
            mixed_v[b], wq_v[...].reshape(heads * hdim, width), (((1,), (1,)), ((), ())),
            preferred_element_type=f32,
        ).astype(bf)
        for h in range(heads):
            a = jnp.dot(q[:, h * hdim:(h + 1) * hdim], uk_v[h], preferred_element_type=f32)
            r = lax.rsqrt(jnp.mean(a * a, axis=-1, keepdims=True) + EPS)
            scaled[b, pl.ds(h * rows, rows), :] = (
                a * r * temps[x * heads + h] / lat
            ).astype(bf)

    gap = lax.broadcasted_iota(jnp.int32, (rows, rows), 1) - lax.broadcasted_iota(
        jnp.int32, (rows, rows), 0
    )

    def task(b, zz):
        bases = [slot(yy, zz, 0) for yy in range(NY)]
        k = jnp.concatenate(
            [kv[pl.ds(base, NX)].reshape(NX * rows, lat) for base in bases], axis=0
        )
        here = bo[slot(y, z, b)]
        seen = [gap <= (here - bo[base + j]) * rows for base in bases for j in range(NX)]
        n_h = 2
        for h0 in range(0, heads, n_h):
            part = pl.ds(h0 * rows, n_h * rows)
            s = lax.dot_general(
                scaled[b, part, :], k, (((1,), (1,)), ((), ())), preferred_element_type=f32
            )
            p = jnp.exp(s)
            p = jnp.concatenate(
                [
                    jnp.concatenate(
                        [
                            jnp.where(
                                seen[j],
                                p[h * rows:(h + 1) * rows, j * rows:(j + 1) * rows],
                                0.0,
                            )
                            for j in range(len(seen))
                        ],
                        axis=1,
                    )
                    for h in range(n_h)
                ],
                axis=0,
            )
            d = p[:, 0:rows]
            for j in range(1, len(seen)):
                d = d + p[:, j * rows:(j + 1) * rows]
            den[b, part, :] += d
            acc[b, part, :] += jnp.dot(p.astype(bf), k, preferred_element_type=f32)

    turns = [(c, w) for c in range(2) for w in (1, 2)]

    def signed(k, w):
        return k if w == 1 else -k

    ask(x)
    spot = mixed_v.at[xs(3), lo]
    net.got(mx["right", 0], spot, at["left"])
    m_up = net.number()
    net.send(m_up, spot, spot, at["right"])
    spot = mixed_v.at[xs(1), hi]
    net.got(mx["left", 1], spot, at["right"])
    m_down = net.number()
    net.send(m_down, spot, spot, at["left"])
    relay(0, 0)
    relay(1, 0)
    piece(1, 0, 1)
    piece(1, 0, 2)
    ended(0, 0)
    ended(1, 0)
    task(x, z)
    piece(1, 1, 1)
    piece(1, 1, 2)
    net.got(mx["right", 1], mixed_v.at[xs(3), hi], at["left"])
    ask(xs(3))
    relay(0, 1)
    relay(0, -1)
    task(xs(3), z)
    net.got(mx["left", 0], mixed_v.at[xs(1), lo], at["right"])
    ask(xs(1))
    relay(1, 1)
    relay(1, -1)
    task(xs(1), z)
    net.got(m_up, mixed_v.at[xs(2), lo], at["left"])
    net.got(m_down, mixed_v.at[xs(2), hi], at["right"])
    ask(xs(2))
    task(xs(2), z)

    rounds = (
        (1, 1, [functools.partial(piece, 2, c, w) for c, w in turns]),
        (1, 2, [functools.partial(relay, c, signed(2, w)) for c, w in turns]),
        (2, 1, [functools.partial(piece, 3, c, w) for c, w in turns]),
        (2, 2, [functools.partial(relay, c, signed(3, w)) for c, w in turns]),
    )
    for k, w, between in rounds:
        for c in range(2):
            ended(c, signed(k, w))
        zz = tile_of(0, signed(k, w))[2]

        def one(b, _, between=between, zz=zz):
            for j, act in enumerate(between):
                pl.when(b == j)(act)
            task(b, zz)
            return 0

        lax.fori_loop(0, NX, one, 0)

    last = [(0, 4), (1, -4)]

    def arrive_three():
        for c, w in turns:
            ended(c, signed(3, w))

    def arrive_four():
        for c, w in turns:
            piece(4, c, w)
        for c, tag in last:
            relay(c, tag)

    def arrive_last():
        for c, tag in last:
            ended(c, tag)

    def last_tiles(b, before=()):
        def one(i, _):
            for j, act in enumerate(before):
                pl.when(i == j)(act)
            task(b, lax.rem(z + 3 + 2 * i - 3 * (i // 2), NZ))
            return 0

        lax.fori_loop(0, 3, one, 0)
        for h in range(heads):
            part = pl.ds(h * rows, rows)
            d = jnp.sum(den[b, part, :], axis=-1, keepdims=True)
            ctx = (acc[b, part, :] / d).astype(bf)
            ho[:, h * hdim:(h + 1) * hdim] = jnp.dot(
                ctx, uv_v[h], preferred_element_type=f32
            ).astype(bf)

    def project():
        return jnp.dot(
            ho[...], wo_v[...].reshape(heads * hdim, width), preferred_element_type=f32
        )

    loads[2].wait()
    last_tiles(xs(2), (arrive_three, arrive_four, arrive_last))
    net.got(wo_far, wo_v.at[wo_other], at["far"])
    po[0] = project().astype(bf)
    out_n = [net.number() for _ in range(4)]
    net.send(out_n[0], po.at[0, lo], passing.at[0], at["right"])
    net.send(out_n[1], po.at[0, hi], passing.at[1], at["left"])
    last_tiles(xs(1))
    net.got(out_n[0], passing.at[0], at["left"])
    res = project()
    po[1, lo] = (res[:half] + passing[0].astype(f32)).astype(bf)
    po[1, hi] = res[half:].astype(bf)
    net.send(out_n[2], po.at[1], landed.at[0], at["right"])
    last_tiles(xs(3))
    net.got(out_n[1], passing.at[1], at["right"])
    res = project()
    po[2, lo] = res[:half].astype(bf)
    po[2, hi] = (res[half:] + passing[1].astype(f32)).astype(bf)
    net.send(out_n[3], po.at[2], landed.at[1], at["left"])
    last_tiles(x)
    res = project()
    net.got(out_n[2], landed.at[0], at["left"])
    net.got(out_n[3], landed.at[1], at["right"])
    out[...] = (res + landed[0].astype(f32) + landed[1].astype(f32)).astype(out.dtype)
    for a, ok, c, n in shifts:
        pl.when(ok)(c.wait_send)
    for dst, n, c, own in moves:
        pl.when(away)(c.wait_send)
    net.drain(at["far"])
    assert net.count == N_COPIES, net.count


N_COPIES = 2 + 3 + 1 + 14 + 7 + 3 + 4 + 56 + 1 + 14 + 48 + 6 + 1 + 4


def tick(bo, temps, depth_temp, embedded, probe, wq, wo, recent, w_latent, w_uk, w_uv):
    rows, width = embedded.shape
    n_heads, hdim, lat = w_uk.shape
    heads = n_heads // NX
    any_ = pl.BlockSpec(memory_space=pl.ANY)
    smem = pl.BlockSpec(memory_space=pltpu.SMEM)
    vmem = pl.BlockSpec(memory_space=pltpu.VMEM)
    bf, f32 = jnp.bfloat16, jnp.float32
    return pl.pallas_call(
        tick_kernel,
        out_shape=jax.ShapeDtypeStruct((rows, width), bf),
        in_specs=[smem] * 3 + [vmem] * 4 + [any_] * 4,
        out_specs=vmem,
        scratch_shapes=[
            pltpu.VMEM(recent.shape, bf),
            pltpu.VMEM((rows, width), f32),
            pltpu.VMEM((rows, 128), f32),
            pltpu.VMEM(w_latent.shape, bf),
            pltpu.VMEM((GROUP,) + wq.shape, bf),
            pltpu.VMEM((GROUP,) + wo.shape, bf),
            pltpu.VMEM((heads, hdim, lat), bf),
            pltpu.VMEM((heads, lat, hdim), bf),
            pltpu.VMEM((NX, rows, width), bf),
            pltpu.VMEM((bo.shape[0], rows, lat), bf),
            pltpu.VMEM((NX, heads * rows, lat), bf),
            pltpu.VMEM((NX, heads * rows, lat), f32),
            pltpu.VMEM((NX, heads * rows, rows), f32),
            pltpu.VMEM((rows, heads * hdim), bf),
            pltpu.VMEM((3, rows, width), bf),
            pltpu.VMEM((2, rows // 2, width), bf),
            pltpu.VMEM((2, rows, width), bf),
            pltpu.SemaphoreType.DMA((N_COPIES,)),
            pltpu.SemaphoreType.DMA((N_COPIES,)),
            pltpu.SemaphoreType.DMA((3,)),
        ],
        compiler_params=pltpu.CompilerParams(
            collective_id=0, has_side_effects=True, vmem_limit_bytes=60 << 20
        ),
        name="tick",
    )(bo, temps, depth_temp, embedded, probe, wq, wo, recent, w_latent, w_uk, w_uv)


def shards(
    embedded, recent, query_depth, depth_temp, w_latent, w_query, w_uk, attn_temp, w_uv,
    w_out, block_offsets,
):
    return tick(
        block_offsets, attn_temp[0], depth_temp, embedded[0], query_depth,
        jnp.swapaxes(w_query[0], 0, 1), w_out[0], recent[0], w_latent[0], w_uk[0], w_uv[0],
    )[None]


def solution(mesh):
    in_specs = (
        P("sec", "seq", None),
        P("sec", None, "seq", None),
        P("sec", None),
        P("sec"),
        P("sec", None, None),
        P("sec", None, "seq"),
        P("sec", None, None, None),
        P("sec", None),
        P("sec", None, None, None),
        P("sec", "seq", None),
        P(),
    )
    return jax.shard_map(
        shards, mesh=mesh, in_specs=in_specs, out_specs=P("sec", "seq", None), check_vma=False
    )
```

time: 209 us -> 182 us (0.87)
  Pallas kernels: 190 us -> 177 us
  other arithmetic: 8.66 us -> 0 us
  local copies, waits for them, and re-layouts: 6.31 us -> 1.92 us
    pallas_call x2 -> x1, Pallas kernels: 190 us -> 177 us  [tick(): pl.pallas_call(tick_kernel, out_shape=jax.ShapeDtypeStruct((rows, width),...]
    reduce_sum x4 -> x0, other arithmetic: 6.95 us -> none  [the longest x1 3.95 us: mix(): logits = temp * scale * jnp.sum(values * probe, axis=-1) * norm]
    dynamic_slice x3 -> x0, local copies, waits for them, and re-layouts: 4.37 us -> none  [the longest x1 1.87 us: shards(): pick(w_uk[0])]
where the time goes in v1:
time: 182 us; the launch traced here: 180 us
  Pallas kernels  177 us (97%)
  local copies, waits for them, and re-layouts  1.92 us (1%)
    pallas_call x1, Pallas kernels, tick(): pl.pallas_call(tick_kernel, out_shape=jax.ShapeDtypeStruct((rows, width),...  177 us

profile of v1, /device:TPU:16, one launch (start us, length us, event | category | flops | bytes accessed | tf_op | source)
XLA Modules:
  0.0 179.7 jit_solution(10440984651087524142)
XLA Ops:
  0.7 177.1 %tick.1 = bf16[128,2304]{1,0:T(8,128)(2,1)} custom-call(s32[64]{0:T(128)} %bo.1, f32[16]{0:T(128)} %bitcast.19, f32[1]{0:T(128)S(6)} %copy.13.depth_temp, bf16[128,2304]{1,0:T(8,128)(2,1)} %bitcast.16, f32[1,2304]{1,0:T(1,128)} %probe.1, bf16[32,2304]{1,0:T(8,128)(2,1)} %bitcast.17, bf16[32,2304]{1,0:T(8,128)(2,1)} %bitcast.18, ...), custom_call_target="tpu_custom_call" | custom-call | tf_op jit(solution)/shard_map/tick/pallas_call | solution.py:517
  177.7 1.9 %copy.14 = bf16[1,128,2304]{2,1,0:T(8,128)(2,1)} copy(bf16[1,128,2304]{2,1,0:T(8,128)(2,1)} %bitcast.11) | data formatting | bytes 1179648

commit v2 on v1

--- a/solution.py
+++ b/solution.py
@@ -102,6 +102,10 @@
     source = x * GROUP + seq // NX
     mine = seq // NX
     away = owner != seq
+    owner_2 = seq_of(1 - rank // NZ, rank % NZ, group)
+    mine_2 = (1 - y) * NZ + z
+    source_2 = x * GROUP + mine_2
+    away_2 = owner_2 != seq
     barrier = pltpu.get_barrier_semaphore()
     names = ("right", "left", "over", "up", "down", "far")
     for name in names:
@@ -115,20 +119,81 @@
     def _():
         pl.semaphore_signal(barrier, inc=1, device_id=(sec, source), device_id_type=MESH)
 
-    pl.semaphore_wait(barrier, len(names) + n_sec - 1 + away.astype(jnp.int32))
+    @pl.when(away_2)
+    def _():
+        pl.semaphore_signal(barrier, inc=1, device_id=(sec, source_2), device_id_type=MESH)
+
+    pl.semaphore_wait(
+        barrier,
+        len(names) + n_sec - 1 + away.astype(jnp.int32) + away_2.astype(jnp.int32),
+    )
 
     net = Net(ssem, rsem)
 
     moves = []
-    for i, (src, dst, base, there) in enumerate(
-        ((wq, wq_v, 0, rank), (wo, wo_v, 0, rank))
-    ):
+
+    def hand_over(src, dst, to, here, off):
         n = net.number()
-        c = net.copy(n, src, dst.at[there], (sec, owner))
-        own = pltpu.make_async_copy(src, dst.at[mine], ssem.at[n])
-        pl.when(away)(c.start)
-        pl.when(jnp.logical_not(away))(own.start)
-        moves.append((dst, n, c, own))
+        c = net.copy(n, src, dst.at[rank], (sec, to))
+        own = pltpu.make_async_copy(src, dst.at[here], ssem.at[n])
+        pl.when(off)(c.start)
+        pl.when(jnp.logical_not(off))(own.start)
+        moves.append((off, c))
+
+        def taken(origin):
+            spot = dst.at[here]
+
+            @pl.when(off)
+            def _():
+                net.copy(n, spot, spot, (sec, origin)).wait_recv()
+
+            pl.when(jnp.logical_not(off))(own.wait)
+            return spot
+
+        return taken
+
+    near_q = hand_over(wq, wq_v, owner, mine, away)
+    other_q = hand_over(wq, wq_v, owner_2, mine_2, away_2)
+    ring_up, ring_down, crossed, ready = {}, {}, {}, []
+
+    def cross(tag, spot):
+        crossed[tag] = net.number()
+        net.send(crossed[tag], spot, spot, at["far"])
+
+    def ring(i, d, k, spot, ways=3):
+        last_up = 4 if d == 0 else 3
+        if ways & 1 and k <= last_up:
+            ring_up[i, d, k] = net.number()
+            net.send(ring_up[i, d, k], spot, spot, at["up"])
+        if ways & 2 and k <= 7 - last_up:
+            ring_down[i, d, k] = net.number()
+            net.send(ring_down[i, d, k], spot, spot, at["down"])
+
+    def ring_step(k, i, dst):
+        for d in range(2):
+            yy = y if d == 0 else 1 - y
+            if (i, d, k) in ring_up:
+                spot = dst.at[yy * NZ + lax.rem(z + NZ - k, NZ)]
+                net.got(ring_up[i, d, k], spot, at["down"])
+                ring(i, d, k + 1, spot, 1)
+                if i == 1:
+                    ready.append((k, spot))
+            if (i, d, k) in ring_down:
+                spot = dst.at[yy * NZ + lax.rem(z + k, NZ)]
+                net.got(ring_down[i, d, k], spot, at["up"])
+                ring(i, d, k + 1, spot, 2)
+                if i == 1:
+                    ready.append((-k, spot))
+
+    def ring_q(k):
+        ring_step(k, 0, wq_v)
+
+    def ring_o(k):
+        ring_step(k, 1, wo_v)
+
+    ring(0, 0, 1, near_q(source))
+    ring(0, 1, 1, other_q(source_2))
+    near_o = hand_over(wo, wo_v, owner, mine, away)
     shifts = []
     for a in range(1, n_sec):
         n = net.number()
@@ -138,47 +203,6 @@
         )
         pl.when(ok)(c.start)
         shifts.append((a, ok, c, n))
-    ring_up, ring_down = {}, {}
-
-    def ring(i, d, k, spot, ways=3):
-        last_up = 4 if d == 0 else 3
-        if ways & 1 and k <= last_up:
-            ring_up[i, d, k] = net.number()
-            net.send(ring_up[i, d, k], spot, spot, at["up"])
-        if ways & 2 and k <= 7 - last_up:
-            ring_down[i, d, k] = net.number()
-            net.send(ring_down[i, d, k], spot, spot, at["down"])
-
-    def ring_step(k):
-        for i, (dst, n, c, own) in enumerate(moves):
-            for d in range(2):
-                yy = y if d == 0 else 1 - y
-                if (i, d, k) in ring_up:
-                    spot = dst.at[yy * NZ + lax.rem(z + NZ - k, NZ)]
-                    net.got(ring_up[i, d, k], spot, at["down"])
-                    ring(i, d, k + 1, spot, 1)
-                if (i, d, k) in ring_down:
-                    spot = dst.at[yy * NZ + lax.rem(z + k, NZ)]
-                    net.got(ring_down[i, d, k], spot, at["up"])
-                    ring(i, d, k + 1, spot, 2)
-
-    q_far = net.number()
-    for i, (dst, n, c, own) in enumerate(moves):
-        spot = dst.at[mine]
-
-        @pl.when(away)
-        def _():
-            net.copy(n, spot, spot, (sec, source)).wait_recv()
-
-        pl.when(jnp.logical_not(away))(own.wait)
-        if i == 0:
-            net.send(q_far, spot, spot, at["far"])
-        ring(i, 0, 1, spot)
-    spot = wq_v.at[(1 - y) * NZ + z]
-    net.got(q_far, spot, at["far"])
-    ring(0, 1, 1, spot)
-    ring_step(1)
-
     asked = probe[...]
     scale = (
         depth_temp[0] * lax.rsqrt(jnp.mean(asked * asked, axis=-1, keepdims=True) + EPS) / width
@@ -202,7 +226,13 @@
         lax.fori_loop(0, rows // step_rows, some, 0)
 
     add_source(lambda part: embedded[part, :], True)
-    ring_step(2)
+    ring_q(1)
+    spot_o = near_o(source)
+    ring(1, 0, 1, spot_o)
+    ready.append((0, spot_o))
+    ring_q(2)
+    ring_o(1)
+    ring_q(3)
     for a, ok, c, n in shifts:
 
         @pl.when(sec >= a)
@@ -283,7 +313,8 @@
                 net.got(table[n], spot, at[back])
                 onward("a", c * NX + i, k + 1, spot, way)
 
-    ring_step(3)
+    ring_q(4)
+    ring_o(2)
     mine_lo, mine_hi = kv.at[slot_me, lo], kv.at[slot_me, hi]
     for name in ("right", "left", "over"):
         ax[name] = net.number()
@@ -315,11 +346,11 @@
         spot = kv.at[slot(1 - y, z, a_x[i]), lo]
         net.got(a_far[i], spot, at["far"])
         onward("a", NX + i, 1, spot)
-    ring_step(4)
-    wo_far = net.number()
-    wo_mine, wo_other = pl.ds(y * NZ, NZ), pl.ds((1 - y) * NZ, NZ)
-    net.send(wo_far, wo_v.at[wo_mine], wo_v.at[wo_mine], at["far"])
-
+
+    ring_o(3)
+    ring_o(4)
+    for tag, spot in ready:
+        cross(tag, spot)
     loads[1].wait()
     acc[...] = jnp.zeros_like(acc)
     den[...] = jnp.zeros_like(den)
@@ -473,7 +504,8 @@
 
     loads[2].wait()
     last_tiles(xs(2), (arrive_three, arrive_four, arrive_last))
-    net.got(wo_far, wo_v.at[wo_other], at["far"])
+    for tag, n in crossed.items():
+        net.got(n, wo_v.at[(1 - y) * NZ + lax.rem(z + NZ - tag, NZ)], at["far"])
     po[0] = project().astype(bf)
     out_n = [net.number() for _ in range(4)]
     net.send(out_n[0], po.at[0, lo], passing.at[0], at["right"])
@@ -497,13 +529,13 @@
     out[...] = (res + landed[0].astype(f32) + landed[1].astype(f32)).astype(out.dtype)
     for a, ok, c, n in shifts:
         pl.when(ok)(c.wait_send)
-    for dst, n, c, own in moves:
-        pl.when(away)(c.wait_send)
+    for off, c in moves:
+        pl.when(off)(c.wait_send)
     net.drain(at["far"])
     assert net.count == N_COPIES, net.count
 
 
-N_COPIES = 2 + 3 + 1 + 14 + 7 + 3 + 4 + 56 + 1 + 14 + 48 + 6 + 1 + 4
+N_COPIES = 3 + 3 + 14 + 7 + 8 + 3 + 4 + 56 + 1 + 14 + 48 + 6 + 4
 
 
 def tick(bo, temps, depth_temp, embedded, probe, wq, wo, recent, w_latent, w_uk, w_uv):

time: 182 us -> 176 us (0.967)
  Pallas kernels: 177 us -> 171 us
    pallas_call x1, Pallas kernels: 177 us -> 171 us  [tick(): pl.pallas_call(tick_kernel, out_shape=jax.ShapeDtypeStruct((rows, width),...]
where the time goes in v2:
time: 176 us; the launch traced here: 174 us
  Pallas kernels  171 us (97%)
  local copies, waits for them, and re-layouts  1.92 us (1%)
    pallas_call x1, Pallas kernels, tick(): pl.pallas_call(tick_kernel, out_shape=jax.ShapeDtypeStruct((rows, width),...  171 us

profile of v2, /device:TPU:16, one launch (start us, length us, event | category | flops | bytes accessed | tf_op | source)
XLA Modules:
  0.0 173.6 jit_solution(8394314933471411117)
XLA Ops:
  0.7 171.0 %tick.1 = bf16[128,2304]{1,0:T(8,128)(2,1)} custom-call(s32[64]{0:T(128)} %bo.1, f32[16]{0:T(128)} %bitcast.19, f32[1]{0:T(128)S(6)} %copy.13.depth_temp, bf16[128,2304]{1,0:T(8,128)(2,1)} %bitcast.16, f32[1,2304]{1,0:T(1,128)} %probe.1, bf16[32,2304]{1,0:T(8,128)(2,1)} %bitcast.17, bf16[32,2304]{1,0:T(8,128)(2,1)} %bitcast.18, ...), custom_call_target="tpu_custom_call" | custom-call | tf_op jit(solution)/shard_map/tick/pallas_call | solution.py:549
  171.7 1.9 %copy.14 = bf16[1,128,2304]{2,1,0:T(8,128)(2,1)} copy(bf16[1,128,2304]{2,1,0:T(8,128)(2,1)} %bitcast.11) | data formatting | bytes 1179648
